TPU v7x, 128 devices: a whole 4x4x4 slice. The times are simulated.
128 devices in a mesh: req: 16 (over z, y), tp: 8 (over x, core).
Axes of the slice: x: 4, y: 4, z: 4, core: 2. Of those that a mesh axis runs over, the one named last changes fastest.
Arguments:
- hidden_in: bfloat16 [4096, 1024], P('req'), may hold values from -42 to 42
- prompt_kv: bfloat16 [2, 128, 512, 1024], P(None, 'req', None, 'tp'), may hold values from -9 to 9
- tail_kv: bfloat16 [2, 4096, 64, 1024], P(None, 'req', None, 'tp'), may hold values from -9 to 9
- group_of: int32 [4096], P('req'), may hold values from 0 to 7
- prompt_len: int32 [128], P('req'), may hold values from 64 to 512, as said below
- tail_len: int32 [4096], P('req'), may hold values from 0 to 63, as said below
- bucket_of: int32 [577], replicated, may hold values from 0 to 31, never falling along the last dimension, each value on 1 to 38 neighbouring positions
- bias_table: float32 [32, 16], P(None, 'tp'), may hold values from -6 to 302
- attn_gain: float32 [1024], replicated, may hold values from 0.1 to 1.9
- w_query: bfloat16 [1024, 1024], P(None, 'tp'), may hold values from -0.1875 to 0.1875
- w_key: bfloat16 [1024, 1024], P(None, 'tp'), may hold values from -0.1875 to 0.1875
- w_value: bfloat16 [1024, 1024], P(None, 'tp'), may hold values from -0.1875 to 0.1875
- w_out: bfloat16 [1024, 1024], P('tp'), may hold values from -0.75 to 0.75
- ffn_gain: float32 [1024], replicated, may hold values from 0.1 to 1.9
- router_weight: bfloat16 [1024, 16], replicated, may hold values from -0.1875 to 0.1875
- expert_ids: int32 [4096, 2], P('req'), may hold values from 0 to 15, all different within a row; in each aligned block of 256 rows (0 to 255, 256 to 511, ...) at most 40 rows name the same one
- w_gate: bfloat16 [16, 1024, 2816], P('req', None, 'tp'), may hold values from -0.1875 to 0.1875
- w_up: bfloat16 [16, 1024, 2816], P('req', None, 'tp'), may hold values from -0.1875 to 0.1875
- w_down: bfloat16 [16, 2816, 1024], P('req', 'tp'), may hold values from -0.109375 to 0.109375
- new_slot: int32 [4096], replicated, may hold values from 0 to 4095, as said below
Outputs:
- out_hidden: bfloat16 [4096, 1024], P('req')
- new_tail_kv: bfloat16 [2, 4096, 64, 1024], P(None, 'req', None, 'tp')
Inputs may be any that keep to these rules, and one draw needn't show every extreme that they name: `expert_ids`: in each replica's aligned block of 256 tokens no expert is named by more than 40 of them, a bound that some block reaches. `new_slot`: A permutation. Exactly 4 requests of each replica are movers; all movers of one replica go to one replica (possibly itself), each taking a slot that a mover of that replica leaves; every other request keeps its slot. `prompt_len`: each replica has a group of 512 rows. `tail_len`: each replica has a request of 63 own rows and one of none.
All inputs are finite; a program needn't handle non-finite values.
Results may differ from a plain program's by a relative error of at most 0.013.
Values may be sent and summed in bfloat16 or wider, within the bound.
A program may use at most 128 MiB of HBM per device.

v0:
```python
import jax
import jax.numpy as jnp
from jax import lax
from jax.sharding import PartitionSpec as P

HD = 64
TOP = 2
MIG = 4
EPS = 1e-06


def rms_scale(values, gain):
    v = values.astype(jnp.float32)
    return (v * lax.rsqrt(jnp.mean(v * v, axis=-1, keepdims=True) + EPS) * gain).astype(
        jnp.bfloat16
    )


def bias_lookup(distance, starts, finish, bias_table):
    within = (distance[..., None] >= starts) & (distance[..., None] < finish)
    return jnp.einsum(
        "rjk,kh->hrj", within.astype(jnp.float32), bias_table, precision=lax.Precision.HIGHEST
    )


def attention(
    hidden_in,
    prompt_kv,
    tail_kv,
    group_of,
    prompt_len,
    tail_len,
    bucket_of,
    bias_table,
    attn_gain,
    w_query,
    w_key,
    w_value,
):
    normed = rms_scale(hidden_in, attn_gain)
    query = jnp.dot(normed, w_query, preferred_element_type=jnp.float32).astype(jnp.bfloat16)
    key_new = jnp.dot(normed, w_key, preferred_element_type=jnp.float32).astype(jnp.bfloat16)
    value_new = jnp.dot(normed, w_value, preferred_element_type=jnp.float32).astype(jnp.bfloat16)
    rows = hidden_in.shape[0]
    heads_here = w_query.shape[1] // HD
    groups_here = prompt_kv.shape[1]
    prompt_rows = prompt_kv.shape[2]
    tail_rows = tail_kv.shape[2]
    span = bucket_of.shape[0]
    buckets = bias_table.shape[0]
    bucket_ids = jnp.arange(buckets, dtype=jnp.int32)
    starts = jnp.sum((bucket_of[:, None] < bucket_ids[None, :]).astype(jnp.int32), axis=0)
    finish = jnp.concatenate([starts[1:], jnp.full((1,), span, jnp.int32)])
    first_bias = jnp.sum(jnp.where((bucket_ids == bucket_of[0])[:, None], bias_table, 0.0), axis=0)
    scale = HD ** (-0.5)
    q = query.reshape(rows, heads_here, HD)
    pk = prompt_kv[0].reshape(groups_here, prompt_rows, heads_here, HD)
    pv = prompt_kv[1].reshape(groups_here, prompt_rows, heads_here, HD)
    tk = tail_kv[0].reshape(rows, tail_rows, heads_here, HD)
    tv = tail_kv[1].reshape(rows, tail_rows, heads_here, HD)
    kn = key_new.reshape(rows, heads_here, HD)
    vn = value_new.reshape(rows, heads_here, HD)
    group_hit = group_of[:, None] == jnp.arange(groups_here, dtype=jnp.int32)[None, :]
    own_len = jnp.sum(jnp.where(group_hit, prompt_len[None, :], 0), axis=1)
    pos = own_len + tail_len
    jpos = jnp.arange(prompt_rows, dtype=jnp.int32)
    pidx = jnp.clip(pos[:, None] - jpos[None, :], 0, span - 1)
    pbias = bias_lookup(pidx, starts, finish, bias_table)
    pmask = group_hit[:, :, None] & (jpos[None, None, :] < own_len[:, None, None])
    ps = (
        jnp.einsum("rhd,gjhd->hrgj", q, pk, preferred_element_type=jnp.float32) * scale
        + pbias[:, :, None, :]
    )
    ps = jnp.where(pmask[None], ps, -jnp.inf)
    tpos = jnp.arange(tail_rows, dtype=jnp.int32)
    tidx = jnp.clip(tail_len[:, None] - tpos[None, :], 0, span - 1)
    tbias = bias_lookup(tidx, starts, finish, bias_table)
    tmask = tpos[None, :] < tail_len[:, None]
    ts = jnp.einsum("rhd,rthd->hrt", q, tk, preferred_element_type=jnp.float32) * scale + tbias
    ts = jnp.where(tmask[None], ts, -jnp.inf)
    ns = (
        jnp.einsum("rhd,rhd->hr", q, kn, preferred_element_type=jnp.float32) * scale
        + first_bias[:, None]
    )
    top = jnp.maximum(jnp.maximum(jnp.max(ps, axis=(2, 3)), jnp.max(ts, axis=2)), ns)
    pe = jnp.exp(ps - top[:, :, None, None])
    te = jnp.exp(ts - top[:, :, None])
    ne = jnp.exp(ns - top)
    total = jnp.sum(pe, axis=(2, 3)) + jnp.sum(te, axis=2) + ne
    pw = (pe / total[:, :, None, None]).astype(jnp.bfloat16)
    tw = (te / total[:, :, None]).astype(jnp.bfloat16)
    nw = (ne / total).astype(jnp.bfloat16)
    head = jnp.einsum("hrgj,gjhd->rhd", pw, pv, preferred_element_type=jnp.float32)
    head = head + jnp.einsum("hrt,rthd->rhd", tw, tv, preferred_element_type=jnp.float32)
    head = head + jnp.einsum("hr,rhd->rhd", nw, vn, preferred_element_type=jnp.float32)
    head_out = head.reshape(rows, heads_here * HD).astype(jnp.bfloat16)
    return (head_out, key_new, value_new, tmask)


def body(
    hidden_in,
    prompt_kv,
    tail_kv,
    group_of,
    prompt_len,
    tail_len,
    bucket_of,
    bias_table,
    attn_gain,
    w_query,
    w_key,
    w_value,
    w_out,
    ffn_gain,
    router_weight,
    expert_ids,
    w_gate,
    w_up,
    w_down,
    new_slot,
):
    head_out, key_new, value_new, tmask = attention(
        hidden_in,
        prompt_kv,
        tail_kv,
        group_of,
        prompt_len,
        tail_len,
        bucket_of,
        bias_table,
        attn_gain,
        w_query,
        w_key,
        w_value,
    )
    rows = hidden_in.shape[0]
    width = hidden_in.shape[1]
    local_idx = jnp.arange(rows, dtype=jnp.int32)
    tail_rows = tail_kv.shape[2]
    write_row = jnp.arange(tail_rows, dtype=jnp.int32)[None, :] == tail_len[:, None]
    fresh = jnp.stack([key_new, value_new])[:, :, None, :]
    tail_new = jnp.where(write_row[None, :, :, None], fresh, tail_kv)
    partial_attn = jnp.dot(head_out, w_out, preferred_element_type=jnp.float32)
    attn = lax.psum(partial_attn, "tp")
    resid = (hidden_in.astype(jnp.float32) + attn).astype(jnp.bfloat16)
    normed2 = rms_scale(resid, ffn_gain)
    logits = jnp.dot(normed2, router_weight, preferred_element_type=jnp.float32)
    experts = router_weight.shape[1]
    expert_range = jnp.arange(experts, dtype=jnp.int32)
    first_hit = expert_ids[:, 0:1] == expert_range[None, :]
    second_hit = expert_ids[:, 1:2] == expert_range[None, :]
    picked_first = jnp.sum(jnp.where(first_hit, logits, 0.0), axis=1)
    picked_second = jnp.sum(jnp.where(second_hit, logits, 0.0), axis=1)
    gate_first = jax.nn.sigmoid(picked_first - picked_second)
    capacity = 5 * rows * TOP // (4 * experts)
    flat_e = expert_ids.reshape(-1)
    onehot = (flat_e[:, None] == expert_range[None, :]).astype(jnp.int32)
    slot_pos = jnp.sum((jnp.cumsum(onehot, axis=0) - 1) * onehot, axis=1)
    target = flat_e * capacity + slot_pos
    placed = (target[:, None] == jnp.arange(experts * capacity, dtype=jnp.int32)[None, :]).astype(
        jnp.bfloat16
    )
    doubled = jnp.repeat(normed2, TOP, axis=0)
    outgoing = (
        jnp.dot(placed.T, doubled, preferred_element_type=jnp.float32)
        .astype(jnp.bfloat16)
        .reshape(experts, capacity, width)
    )
    gate_mat = w_gate[0]
    up_mat = w_up[0]
    down_mat = w_down[0]
    received = lax.all_to_all(outgoing, "req", split_axis=0, concat_axis=0, tiled=True)
    flat = received.reshape(-1, received.shape[-1])
    gate_h = jnp.dot(flat, gate_mat, preferred_element_type=jnp.float32)
    up_h = jnp.dot(flat, up_mat, preferred_element_type=jnp.float32)
    act = (jax.nn.gelu(gate_h, approximate=True) * up_h).astype(jnp.bfloat16)
    summed = lax.psum(
        jnp.dot(act, down_mat, preferred_element_type=jnp.float32).astype(jnp.bfloat16), "tp"
    )
    back = summed.reshape(received.shape)
    result = lax.all_to_all(back, "req", split_axis=0, concat_axis=0, tiled=True)
    pair_out = jnp.dot(
        placed, result.reshape(experts * capacity, width), preferred_element_type=jnp.float32
    ).reshape(rows, TOP, width)
    mixed = (
        resid.astype(jnp.float32)
        + gate_first[:, None] * pair_out[:, 0]
        + (1.0 - gate_first)[:, None] * pair_out[:, 1]
    ).astype(jnp.bfloat16)
    replicas = lax.axis_size("req")
    me = lax.axis_index("req")
    total_reqs = new_slot.shape[0]
    everyone = jnp.arange(total_reqs, dtype=jnp.int32)
    leaving_all = new_slot // rows != everyone // rows
    rank_all = (
        jnp.cumsum(leaving_all.reshape(replicas, rows).astype(jnp.int32), axis=1) - 1
    ).reshape(-1)
    source_of = jnp.zeros((total_reqs,), jnp.int32).at[new_slot].set(everyone)
    first_slot = me * rows
    leaving = lax.dynamic_slice_in_dim(leaving_all, first_slot, rows, 0)
    my_rank = lax.dynamic_slice_in_dim(rank_all, first_slot, rows, 0)
    send_idx = (
        jnp.zeros((MIG,), jnp.int32)
        .at[jnp.where(leaving, my_rank, MIG)]
        .set(local_idx, mode="drop")
    )
    send_rows = mixed[send_idx]
    send_tail = jnp.swapaxes(tail_new[:, send_idx], 0, 1)
    got_rows, got_tail = (
        lax.all_gather(send_rows, "req", axis=0, tiled=True),
        lax.all_gather(send_tail, "req", axis=0, tiled=True),
    )
    count = jnp.sum(leaving.astype(jnp.int32))
    vacated = jnp.where(jnp.arange(MIG, dtype=jnp.int32) < count, send_idx, rows)
    source = source_of[first_slot + jnp.minimum(vacated, rows - 1)]
    position = source // rows * MIG + rank_all[source]
    position = jnp.clip(position, 0, got_rows.shape[0] - 1)
    out_hidden = mixed.at[vacated].set(got_rows[position], mode="drop")
    new_tail_kv = tail_new.at[:, vacated].set(jnp.swapaxes(got_tail[position], 0, 1), mode="drop")
    return (out_hidden, new_tail_kv)


def solution(mesh):
    return jax.shard_map(
        body,
        mesh=mesh,
        in_specs=(
            P("req", None),
            P(None, "req", None, "tp"),
            P(None, "req", None, "tp"),
            P("req"),
            P("req"),
            P("req"),
            P(),
            P(None, "tp"),
            P(),
            P(None, "tp"),
            P(None, "tp"),
            P(None, "tp"),
            P("tp", None),
            P(),
            P(),
            P("req", None),
            P("req", None, "tp"),
            P("req", None, "tp"),
            P("req", "tp", None),
            P(),
        ),
        out_specs=(P("req", None), P(None, "req", None, "tp")),
        check_vma=False,
    )
```

profile of v0, /device:TPU:6, one launch (start us, length us, event | category | flops | bytes accessed | tf_op | source)
XLA Modules:
  0.0 309.5 jit_solution(10653071250375701447)
XLA Ops:
  8.1 1.3 iota_compare_fusion.11
  9.3 0.8 select_reduce_fusion.2
  10.3 0.7 add.171
  10.9 1.3 iota_compare_fusion.5
  12.2 1.3 subtract_clamp_fusion.1
  13.6 0.8 convert_reduce_fusion
  14.4 1.2 slice.45
  15.9 6.9 %fusion.8 = f32[2,256,512]{2,0,1:T(2,128)S(1)} fusion(s32[256,512]{1,0:T(8,128)S(1)} %subtract_clamp_fusion, s32[32]{0:T(128)S(1)} %pad_add_fusion, s32[32]{0:T(128)S(1)} %convert_reduce_fusion, f32[32,2]{0,1:T(2,128)} %param.27), kind=kOutput, calls=%fused_computation.35 | convolution fusion | flops 113246208 | bytes 1573376 | tf_op jit(solution)/shard_map/rjk,kh->hrj/dot_general | solution.py:21
  23.2 1.2 fusion.90
  24.5 1.3 copy.113
  25.8 6.5 %fusion.89 = (bf16[1,256,64,128]{3,2,1,0:T(8,128)(2,1)}, bf16[1,256,64,128]{3,2,1,0:T(8,128)(2,1)}) fusion(bf16[2,256,64,128]{3,2,1,0:T(8,128)(2,1)} %param.22), kind=kLoop, calls=%fused_computation.187 | loop fusion | bytes 16777216 | tf_op jit(solution)/shard_map/slice | solution.py:59
  32.3 7.0 %copy.114 = bf16[1,256,64,128]{1,3,2,0:T(8,128)(2,1)} copy(bf16[1,256,64,128]{3,2,1,0:T(8,128)(2,1)} %get-tuple-element.12) | data formatting | bytes 8388608
  39.8 1.1 convolution_convert_fusion.3
  41.6 1.3 broadcast_and_fusion
  42.9 3.7 %multiply_reduce_fusion.1 = f32[2,256,64]{1,0,2:T(2,128)S(1)} fusion(bf16[2,256,64,64]{1,2,0,3:T(8,128)(2,1)} %bitcast.145, f32[2,256,64]{1,2,0:T(8,128)S(1)} %get-tuple-element.27), kind=kLoop, calls=%fused_computation.13 | loop fusion | flops 6258688 | bytes 4456448 | tf_op jit(solution)/shard_map/rhd,rthd->hrt/dot_general | solution.py:79
  46.7 0.9 fusion.92
  47.6 2.2 fusion.5
  49.9 2.7 fusion.4
  53.4 0.7 convert_bitcast_fusion
  54.7 6.9 %copy.116 = bf16[1,256,64,128]{1,3,2,0:T(8,128)(2,1)} copy(bf16[1,256,64,128]{3,2,1,0:T(8,128)(2,1)} %get-tuple-element.13) | data formatting | bytes 8388608
  61.6 2.0 convolution_convert_fusion.2
  63.6 2.3 copy.115
  65.9 3.2 %multiply_reduce_fusion = f32[256,2,64]{0,2,1:T(8,128)S(1)} fusion(bf16[256,2,64,64]{0,3,1,2:T(8,128)(2,1)} %bitcast.146, f32[256,2,64]{0,1,2:T(2,128)S(1)} %bitcast_convert_fusion), kind=kLoop, calls=%fused_computation.12 | loop fusion | flops 6258688 | bytes 4456448 | tf_op jit(solution)/shard_map/hrt,rthd->rhd/dot_general | solution.py:94
  69.2 5.1 %fusion.19 = bf16[256,2,64]{0,2,1:T(8,128)(2,1)S(1)} fusion(f32[256,2,64]{0,2,1:T(8,128)S(1)} %multiply_reduce_fusion, f32[2,256,8,512]{3,1,2,0:T(8,128)} %copy-done.1, f32[2,256]{1,0:T(2,128)S(1)} %copy-done.18, f32[2,256]{1,0:T(2,128)S(1)} %copy-done.13, f32[2,256,512]{2,1,0:T(8,128)S(1)} %copy.78, pred[256,8,512]{2,0,1:T(8,128)(4,1)S(1)} %broadcast_and_fusion, ...), kind=kOutput, calls=%fused_computation.52 | convolution fusion | flops 281182208 | bytes 11802624 | tf_op jit(solution)/shard_map/hrgj,gjhd->rhd/dot_general | solution.py:93
  74.3 1.3 fusion.93
  76.1 1.2 reduce-window.14
  77.6 60.5 %all-reduce.3.cloned.1.call-done = f32[256,1024]{1,0:T(8,128)} async-done(((f32[256,1024]{1,0:T(8,128)}), f32[256,1024]{1,0:T(8,128)}) %all-reduce.3.cloned.1.call-update) | async-done | bytes 1048592 | tf_op jit(solution)/shard_map/psum | solution.py:144
  138.1 1.5 fusion.24
  140.4 1.2 reshape.353
  141.6 3.2 %convolution_convert_fusion.1 = bf16[640,1024]{1,0:T(8,128)(2,1)} fusion(bf16[512,1024]{1,0:T(8,128)(2,1)} %reshape.353, s32[512]{0:T(512)S(1)} %multiply_add_fusion), kind=kOutput, calls=%fused_computation.28 | convolution fusion | flops 672071680 | bytes 2361344 | tf_op jit(solution)/shard_map/dot_general | solution.py:165
  144.9 7.0 %all-to-all-start = ((bf16[16,40,1024]{2,1,0:T(8,128)(2,1)}), bf16[16,40,1024]{2,1,0:T(8,128)(2,1)S(1)}, u32[]{:S(2)}, u32[]{:S(2)}) async-start(bf16[16,40,1024]{2,1,0:T(8,128)(2,1)} %bitcast.149), calls=%async_computation | async-start | bytes 2621440 | tf_op jit(solution)/shard_map/all_to_all | solution.py:172
  153.2 0.7 convert_reduce_fusion.1
  153.9 1.4 scatter_custom_fusion
  155.3 0.7 compare_select_fusion.2
  156.0 20.2 %all-to-all-done = bf16[16,40,1024]{2,1,0:T(8,128)(2,1)S(1)} async-done(((bf16[16,40,1024]{2,1,0:T(8,128)(2,1)}), bf16[16,40,1024]{2,1,0:T(8,128)(2,1)S(1)}, u32[]{:S(2)}, u32[]{:S(2)}) %all-to-all-start) | async-done | bytes 1310752 | tf_op jit(solution)/shard_map/all_to_all | solution.py:172
  176.1 2.8 fusion.48
  178.9 4.3 %convolution_convert_fusion = bf16[640,1024]{1,0:T(8,128)(2,1)} fusion(bf16[640,1024]{1,0:T(8,128)(2,1)S(1)} %bitcast.148, f32[640,352]{0,1:T(8,128)} %fusion.48, bf16[1,352,1024]{2,1,0:T(8,128)(2,1)S(1)} %copy-done, bf16[1,1024,352]{1,2,0:T(8,128)(2,1)} %param.37), kind=kOutput, calls=%fused_computation.27 | convolution fusion | flops 925655040 | bytes 4964352 | tf_op jit(solution)/shard_map/dot_general | solution.py:178
  183.3 8.3 %broadcast_select_fusion = bf16[2,256,64,128]{3,2,1,0:T(8,128)(2,1)} fusion(bf16[2,256,64,128]{3,2,1,0:T(8,128)(2,1)} %param.22, pred[256,64]{1,0:T(8,128)(4,1)S(1)} %copy.89, bf16[2,256,128]{2,1,0:T(8,128)(2,1)S(1)} %copy.90), kind=kLoop, calls=%fused_computation.20 | loop fusion | flops 4194304 | bytes 16924672 | tf_op jit(solution)/shard_map/jit(_where)/select_n | solution.py:142
  191.5 4.7 %gather_fusion.3 = bf16[4,2,64,128]{3,2,1,0:T(8,128)(2,1)} fusion(bf16[2,256,64,128]{3,2,1,0:T(8,128)(2,1)} %broadcast_select_fusion, s32[1024]{0:T(1024)S(1)} %pad_clamp_fusion.3), kind=kCustom, calls=%fused_computation.4 | custom fusion | bytes 262160 | tf_op jit(solution)/shard_map/gather | solution.py:208
  196.5 15.5 %scatter_custom_fusion.1 = s32[4096]{0:T(1024)S(1)} fusion(s32[4096]{0:T(1024)S(1)} %add_select_fusion.1, s32[4096]{0:T(1024)S(1)} %iota.80, s32[]{:T(128)} %constant.36.clone.1), kind=kCustom, calls=%fused_computation.136 | custom fusion | bytes 16388 | tf_op jit(solution)/shard_map/scatter | solution.py:198
  212.7 28.9 %all-reduce.5.cloned.1.call-done = bf16[16,40,1024]{2,1,0:T(8,128)(2,1)} async-done(((bf16[16,40,1024]{2,1,0:T(8,128)(2,1)}), bf16[16,40,1024]{2,1,0:T(8,128)(2,1)}) %all-reduce.5.cloned.1.call-update) | async-done | bytes 1310736 | tf_op jit(solution)/shard_map/psum | solution.py:177
  241.6 7.0 %all-to-all-start.1 = ((bf16[16,40,1024]{2,1,0:T(8,128)(2,1)}), bf16[16,40,1024]{2,1,0:T(8,128)(2,1)S(1)}, u32[]{:S(2)}, u32[]{:S(2)}) async-start(bf16[16,40,1024]{2,1,0:T(8,128)(2,1)} %all-reduce.5.cloned.1.call-done), calls=%async_computation.1 | async-start | bytes 2621440 | tf_op jit(solution)/shard_map/all_to_all | solution.py:181
  249.6 23.0 %all-to-all-done.1 = bf16[16,40,1024]{2,1,0:T(8,128)(2,1)S(1)} async-done(((bf16[16,40,1024]{2,1,0:T(8,128)(2,1)}), bf16[16,40,1024]{2,1,0:T(8,128)(2,1)S(1)}, u32[]{:S(2)}, u32[]{:S(2)}) %all-to-all-start.1) | async-done | bytes 1310752 | tf_op jit(solution)/shard_map/all_to_all | solution.py:181
  272.7 1.0 fusion.10
  274.5 22.0 %all-gather.1 = bf16[16,4,1024]{2,1,0:T(4,128)(2,1)S(1)} all-gather(bf16[1,4,1024]{2,1,0:T(4,128)(2,1)S(1)} %bitcast.160), channel_id=2, replica_groups=mesh['req'=16,'tp'=8] {'req'}, dimensions={0}, use_global_device_ids=true | all-gather | bytes 139264 | tf_op jit(solution)/shard_map/all_gather | solution.py:210
  296.6 1.0 scatter_custom_fusion.2
  297.7 2.3 gather_fusion.4
  300.0 2.0 scatter_fusion
  (126 shorter events, 9.2 us)
Async XLA Ops:
  8.0 170.9 %copy-start = (bf16[1,352,1024]{2,1,0:T(8,128)(2,1)S(1)}, bf16[1,352,1024]{2,1,0:T(8,128)(2,1)}, u32[]{:S(2)}) copy-start(bf16[1,352,1024]{2,1,0:T(8,128)(2,1)} %param.38) | copy-start | bytes 2162692
  8.0 130.1 %all-reduce.3.cloned.1.call-start = ((), (), s32[]{:S(2)}) async-start(), calls=%async_computation.2 | async-start | bytes 2097152 | tf_op jit(solution)/shard_map/psum | solution.py:144
  14.4 8.4 %copy-start.24 = (s32[32]{0:T(128)}, s32[32]{0:T(128)S(1)}, u32[]{:S(2)}) copy-start(s32[32]{0:T(128)S(1)} %convert_reduce_fusion) | copy-start | bytes 388
  15.9 6.9 %copy-start.29 = (s32[32]{0:T(128)}, s32[32]{0:T(128)S(1)}, u32[]{:S(2)}) copy-start(s32[32]{0:T(128)S(1)} %pad_add_fusion) | copy-start | bytes 388
  15.9 7.1 %copy-start.3 = (bf16[256,1024]{1,0:T(8,128)(2,1)S(1)}, bf16[256,1024]{1,0:T(8,128)(2,1)}, u32[]{:S(2)}) copy-start(bf16[256,1024]{1,0:T(8,128)(2,1)} %param.20) | copy-start | bytes 1572868
  15.9 7.3 %copy-start.2 = (bf16[2,8,512,128]{3,2,1,0:T(8,128)(2,1)S(1)}, bf16[2,8,512,128]{3,2,1,0:T(8,128)(2,1)}, u32[]{:S(2)}) copy-start(bf16[2,8,512,128]{3,2,1,0:T(8,128)(2,1)} %param.21) | copy-start | bytes 6291460
  23.2 16.1 %copy-start.23 = (f32[256]{0:T(256)}, f32[256]{0:T(256)S(1)}, u32[]{:S(2)}) copy-start(f32[256]{0:T(256)S(1)} %add_rsqrt_fusion.1) | copy-start | bytes 3076
  32.3 7.0 %copy-start.26 = (bf16[1024,128]{1,0:T(8,128)(2,1)S(1)}, bf16[1024,128]{1,0:T(8,128)(2,1)}, u32[]{:S(2)}) copy-start(bf16[1024,128]{1,0:T(8,128)(2,1)} %param.29) | copy-start | bytes 786436
  32.3 7.0 %copy-start.28 = (f32[1024]{0:T(1024)S(1)}, f32[1024]{0:T(1024)}, u32[]{:S(2)}) copy-start(f32[1024]{0:T(1024)} %param.28) | copy-start | bytes 12292
  32.3 7.5 %copy-start.27 = (bf16[1024,128]{1,0:T(8,128)(2,1)S(1)}, bf16[1024,128]{1,0:T(8,128)(2,1)}, u32[]{:S(2)}) copy-start(bf16[1024,128]{1,0:T(8,128)(2,1)} %param.30) | copy-start | bytes 786436
  32.3 9.2 %copy-start.21 = (f32[32,2]{0,1:T(2,128)S(1)}, f32[32,2]{0,1:T(2,128)}, u32[]{:S(2)}) copy-start(f32[32,2]{0,1:T(2,128)} %param.27) | copy-start | bytes 772
  39.3 7.3 %copy-start.8 = (s32[256,64]{0,1:T(8,128)S(1)}, s32[256,64]{0,1:T(8,128)}, u32[]{:S(2)}) copy-start(s32[256,64]{0,1:T(8,128)} %subtract_clamp_fusion.1) | copy-start | bytes 196612
  39.3 7.3 %copy-start.16 = (pred[256,64]{0,1:T(8,128)(4,1)S(1)}, pred[256,64]{0,1:T(8,128)(4,1)}, u32[]{:S(2)}) copy-start(pred[256,64]{0,1:T(8,128)(4,1)} %get-tuple-element.21) | copy-start | bytes 49156
  39.3 7.3 %copy-start.22 = (f32[32,2]{0,1:T(2,128)S(1)}, f32[32,2]{0,1:T(2,128)}, u32[]{:S(2)}) copy-start(f32[32,2]{0,1:T(2,128)} %param.27) | copy-start | bytes 772
  39.3 7.3 %copy-start.25 = (s32[32]{0:T(128)S(1)}, s32[32]{0:T(128)}, u32[]{:S(2)}) copy-start(s32[32]{0:T(128)} %copy-done.24) | copy-start | bytes 388
  39.4 7.3 %copy-start.30 = (s32[32]{0:T(128)S(1)}, s32[32]{0:T(128)}, u32[]{:S(2)}) copy-start(s32[32]{0:T(128)} %copy-done.29) | copy-start | bytes 388
  40.8 6.8 %copy-start.4 = (bf16[1,8,512,128]{2,3,1,0:T(8,128)(2,1)S(1)}, bf16[1,8,512,128]{2,3,1,0:T(8,128)(2,1)}, u32[]{:S(2)}) copy-start(bf16[1,8,512,128]{2,3,1,0:T(8,128)(2,1)} %copy.113) | copy-start | bytes 3145732
  49.9 3.4 %copy-start.1 = (f32[2,256,8,512]{3,1,2,0:T(8,128)}, f32[2,256,8,512]{3,1,2,0:T(8,128)S(1)}, u32[]{:S(2)}) copy-start(f32[2,256,8,512]{3,1,2,0:T(8,128)S(1)} %get-tuple-element.26) | copy-start | bytes 25165828
  49.9 4.1 %copy-start.12 = (f32[2,256]{1,0:T(2,128)}, f32[2,256]{1,0:T(2,128)S(1)}, u32[]{:S(2)}) copy-start(f32[2,256]{1,0:T(2,128)S(1)} %maximum_maximum_fusion) | copy-start | bytes 6148
  54.1 0.6 copy-start.17
  65.8 3.2 %copy-start.5 = (bf16[1,8,512,128]{2,3,1,0:T(8,128)(2,1)S(1)}, bf16[1,8,512,128]{2,3,1,0:T(8,128)(2,1)}, u32[]{:S(2)}) copy-start(bf16[1,8,512,128]{2,3,1,0:T(8,128)(2,1)} %copy.115) | copy-start | bytes 3145732
  65.8 3.2 %copy-start.10 = (bf16[256,128]{0,1:T(8,128)(2,1)S(1)}, bf16[256,128]{0,1:T(8,128)(2,1)}, u32[]{:S(2)}) copy-start(bf16[256,128]{0,1:T(8,128)(2,1)} %convolution_convert_fusion.2) | copy-start | bytes 196612
  65.8 3.3 %copy-start.13 = (f32[2,256]{1,0:T(2,128)S(1)}, f32[2,256]{1,0:T(2,128)}, u32[]{:S(2)}) copy-start(f32[2,256]{1,0:T(2,128)} %copy-done.12) | copy-start | bytes 6148
  65.8 3.3 %copy-start.18 = (f32[2,256]{1,0:T(2,128)S(1)}, f32[2,256]{1,0:T(2,128)}, u32[]{:S(2)}) copy-start(f32[2,256]{1,0:T(2,128)} %copy-done.17) | copy-start | bytes 6148
  65.9 3.3 %copy-start.20 = (f32[256,2]{0,1:T(2,128)S(1)}, f32[256,2]{0,1:T(2,128)}, u32[]{:S(2)}) copy-start(f32[256,2]{0,1:T(2,128)} %get-tuple-element.10) | copy-start | bytes 6148
  69.1 5.2 %copy-start.7 = (bf16[128,1024]{1,0:T(8,128)(2,1)S(1)}, bf16[128,1024]{1,0:T(8,128)(2,1)}, u32[]{:S(2)}) copy-start(bf16[128,1024]{1,0:T(8,128)(2,1)} %param.32) | copy-start | bytes 786436
  69.1 6.5 %copy-start.15 = (s32[256,2]{0,1:T(2,128)S(1)}, s32[256,2]{0,1:T(2,128)}, u32[]{:S(2)}) copy-start(s32[256,2]{0,1:T(2,128)} %param.35) | copy-start | bytes 6148
  74.3 65.3 %copy-start.19 = (f32[1024]{0:T(1024)S(1)}, f32[1024]{0:T(1024)}, u32[]{:S(2)}) copy-start(f32[1024]{0:T(1024)} %param.33) | copy-start | bytes 12292
  140.4 11.6 %copy-start.9 = (s32[4096]{0:T(1024)S(1)}, s32[4096]{0:T(1024)}, u32[]{:S(2)}) copy-start(s32[4096]{0:T(1024)} %param.39) | copy-start | bytes 49156
  140.4 12.5 %copy-start.11 = (bf16[256,128]{0,1:T(8,128)(2,1)S(1)}, bf16[256,128]{0,1:T(8,128)(2,1)}, u32[]{:S(2)}) copy-start(bf16[256,128]{0,1:T(8,128)(2,1)} %convolution_convert_fusion.2) | copy-start | bytes 196612
  144.9 31.2 %all-to-all-start = ((bf16[16,40,1024]{2,1,0:T(8,128)(2,1)}), bf16[16,40,1024]{2,1,0:T(8,128)(2,1)S(1)}, u32[]{:S(2)}, u32[]{:S(2)}) async-start(bf16[16,40,1024]{2,1,0:T(8,128)(2,1)} %bitcast.149), calls=%async_computation | async-start | bytes 2621440 | tf_op jit(solution)/shard_map/all_to_all | solution.py:172
  151.9 89.7 %all-reduce.5.cloned.1.call-start = ((), (), s32[]{:S(2)}) async-start(), calls=%async_computation.3 | async-start | bytes 2621440 | tf_op jit(solution)/shard_map/psum | solution.py:177
  183.2 114.4 %all-gather.4.cloned.1.call-start = ((), (), s32[]{:S(2)}) async-start(), calls=%async_computation.4 | async-start | bytes 2228224 | tf_op jit(solution)/shard_map/all_gather | solution.py:211
  191.5 57.8 %copy-start.14 = (bf16[1024,16]{0,1:T(8,128)(2,1)S(1)}, bf16[1024,16]{0,1:T(8,128)(2,1)}, u32[]{:S(2)}) copy-start(bf16[1024,16]{0,1:T(8,128)(2,1)} %param.34) | copy-start | bytes 98308
  241.6 31.1 %all-to-all-start.1 = ((bf16[16,40,1024]{2,1,0:T(8,128)(2,1)}), bf16[16,40,1024]{2,1,0:T(8,128)(2,1)S(1)}, u32[]{:S(2)}, u32[]{:S(2)}) async-start(bf16[16,40,1024]{2,1,0:T(8,128)(2,1)} %all-reduce.5.cloned.1.call-done), calls=%async_computation.1 | async-start | bytes 2621440 | tf_op jit(solution)/shard_map/all_to_all | solution.py:181
  297.6 4.4 %copy-start.6 = (bf16[256,1024]{1,0:T(8,128)(2,1)}, bf16[256,1024]{1,0:T(8,128)(2,1)S(1)}, u32[]{:S(2)}) copy-start(bf16[256,1024]{1,0:T(8,128)(2,1)S(1)} %scatter_custom_fusion.2) | copy-start | bytes 1572868
Sparse Core Ops, SparseCore 0:
  75.7 62.3 all-reduce.2
  183.3 58.1 all-reduce.4
Sparse Core Ops, SparseCore 1:
  196.3 42.1 all-gather.3
where the time goes:
time: 311 us; the launch traced here: 309 us
  waiting for transfers between devices  133 us (43%)
  local copies, waits for them, and re-layouts  59.9 us (19%)
  other arithmetic  33 us (11%)
  matrix products  31.5 us (10%)
  blocking collectives  22 us (7%)
  between operations  16.2 us (5%)
  starting transfers between devices  14.1 us (5%)
    psum x1, waiting for transfers between devices, body(): attn = lax.psum(partial_attn, 'tp')  60.5 us
    psum x1, waiting for transfers between devices, body(): lax.psum(jnp.dot(act, down_mat, preferred_element_type=jnp.float32).astyp...  28.9 us
    all_to_all x1, waiting for transfers between devices, body(): lax.all_to_all(back, 'req', split_axis=0, concat_axis=0, tiled=True)  23 us
    all_gather x1, blocking collectives, body(): lax.all_gather(send_rows, 'req', axis=0, tiled=True)  22 us
    all_to_all x1, waiting for transfers between devices, body(): lax.all_to_all(outgoing, 'req', split_axis=0, concat_axis=0, tiled=True)  20.2 us
    unnamed x68, local copies, waits for them, and re-layouts  18.9 us
    scatter x1, local copies, waits for them, and re-layouts, body(): source_of = jnp.zeros((total_reqs,), jnp.int32).at[new_slot].set(everyone)  15.5 us
    select_n x1, other arithmetic, body(): tail_new = jnp.where(write_row[None, :, :, None], fresh, tail_kv)  8.26 us
  transfers between devices with their start and end apart: 5, of which 4 were waited for; matrix products, arithmetic and copies ran while one was open for 13% of the time, Pallas kernels for 0%

commit v1 on v0

--- a/solution.py
+++ b/solution.py
@@ -7,6 +7,14 @@
 TOP = 2
 MIG = 4
 EPS = 1e-06
+
+
+def add_in_pairs(x, mesh_axis):
+    size, acc = (lax.axis_size(mesh_axis), x)
+    for far in [1 << k for k in range(size.bit_length() - 1)]:
+        pairs = [(i, i ^ far) for i in range(size)]
+        acc = acc + lax.ppermute(acc, mesh_axis, pairs)
+    return acc
 
 
 def rms_scale(values, gain):
@@ -141,7 +149,7 @@
     fresh = jnp.stack([key_new, value_new])[:, :, None, :]
     tail_new = jnp.where(write_row[None, :, :, None], fresh, tail_kv)
     partial_attn = jnp.dot(head_out, w_out, preferred_element_type=jnp.float32)
-    attn = lax.psum(partial_attn, "tp")
+    attn = add_in_pairs(partial_attn, "tp")
     resid = (hidden_in.astype(jnp.float32) + attn).astype(jnp.bfloat16)
     normed2 = rms_scale(resid, ffn_gain)
     logits = jnp.dot(normed2, router_weight, preferred_element_type=jnp.float32)

time: 311 us -> 291 us (0.936)
  waiting for transfers between devices: 133 us -> 113 us
  starting transfers between devices: 14.1 us -> 17.5 us
    psum x1 -> x0, waiting for transfers between devices: 60.5 us -> none  [body(): attn = lax.psum(partial_attn, 'tp')]
    ppermute x0 -> x3, waiting for transfers between devices: none -> 49.6 us  [add_in_pairs(): acc = acc + lax.ppermute(acc, mesh_axis, pairs)]
    all_to_all x1, waiting for transfers between devices: 20.2 us -> 14.8 us  [body(): lax.all_to_all(outgoing, 'req', split_axis=0, concat_axis=0, tiled=True)]
    all_to_all x1, waiting for transfers between devices: 23 us -> 18.9 us  [body(): lax.all_to_all(back, 'req', split_axis=0, concat_axis=0, tiled=True)]
    unnamed x68 -> x48, local copies, waits for them, and re-layouts: 18.9 us -> 19.2 us
  transfers between devices with their start and end apart: 5 -> 7, of which waited for: 4 -> 6; matrix products, arithmetic and copies ran while one was open for 13% -> 14% of each run, Pallas kernels for 0% -> 0%
where the time goes in v1:
time: 291 us; the launch traced here: 289 us
  waiting for transfers between devices  113 us (39%)
  local copies, waits for them, and re-layouts  60.2 us (21%)
  other arithmetic  30.9 us (11%)
  matrix products  29.8 us (10%)
  blocking collectives  22 us (8%)
  starting transfers between devices  17.5 us (6%)
  between operations  16.1 us (6%)
    ppermute x3, waiting for transfers between devices, add_in_pairs(): acc = acc + lax.ppermute(acc, mesh_axis, pairs)  49.6 us
    psum x1, waiting for transfers between devices, body(): lax.psum(jnp.dot(act, down_mat, preferred_element_type=jnp.float32).astyp...  29.4 us
    all_gather x1, blocking collectives, body(): lax.all_gather(send_rows, 'req', axis=0, tiled=True)  22 us
    unnamed x48, local copies, waits for them, and re-layouts  19.2 us
    all_to_all x1, waiting for transfers between devices, body(): lax.all_to_all(back, 'req', split_axis=0, concat_axis=0, tiled=True)  18.9 us
    scatter x1, local copies, waits for them, and re-layouts, body(): source_of = jnp.zeros((total_reqs,), jnp.int32).at[new_slot].set(everyone)  15.5 us
    all_to_all x1, waiting for transfers between devices, body(): lax.all_to_all(outgoing, 'req', split_axis=0, concat_axis=0, tiled=True)  14.8 us
    select_n x1, other arithmetic, body(): tail_new = jnp.where(write_row[None, :, :, None], fresh, tail_kv)  8.07 us
  transfers between devices with their start and end apart: 7, of which 6 were waited for; matrix products, arithmetic and copies ran while one was open for 14% of the time, Pallas kernels for 0%

profile of v1, /device:TPU:6, one launch (start us, length us, event | category | flops | bytes accessed | tf_op | source)
XLA Modules:
  0.0 289.4 jit_solution(4810587636384097016)
XLA Ops:
  8.0 0.8 iota_compare_fusion.11
  8.8 0.8 select_reduce_fusion.2
  10.4 0.7 iota_compare_fusion.5
  11.1 1.3 subtract_clamp_fusion.1
  12.4 0.8 convert_reduce_fusion
  13.2 1.2 slice.45
  14.8 6.9 %fusion.8 = f32[2,256,512]{2,0,1:T(2,128)S(1)} fusion(s32[256,512]{1,0:T(8,128)S(1)} %subtract_clamp_fusion, s32[32]{0:T(128)S(1)} %pad_add_fusion, s32[32]{0:T(128)S(1)} %convert_reduce_fusion, f32[32,2]{0,1:T(2,128)} %param.27), kind=kOutput, calls=%fused_computation.35 | convolution fusion | flops 113246208 | bytes 1573376 | tf_op jit(solution)/shard_map/rjk,kh->hrj/dot_general | solution.py:29
  22.1 1.2 fusion.90
  23.3 1.3 copy.113
  24.6 6.5 %fusion.89 = (bf16[1,256,64,128]{3,2,1,0:T(8,128)(2,1)}, bf16[1,256,64,128]{3,2,1,0:T(8,128)(2,1)}) fusion(bf16[2,256,64,128]{3,2,1,0:T(8,128)(2,1)} %param.22), kind=kLoop, calls=%fused_computation.187 | loop fusion | bytes 16777216 | tf_op jit(solution)/shard_map/slice | solution.py:67
  31.2 7.0 %copy.114 = bf16[1,256,64,128]{1,3,2,0:T(8,128)(2,1)} copy(bf16[1,256,64,128]{3,2,1,0:T(8,128)(2,1)} %get-tuple-element.12) | data formatting | bytes 8388608
  39.0 0.7 iota_compare_fusion.12
  40.5 3.7 %multiply_reduce_fusion.1 = f32[2,256,64]{1,0,2:T(2,128)S(1)} fusion(bf16[2,256,64,64]{1,2,0,3:T(8,128)(2,1)} %bitcast.145, f32[2,256,64]{1,2,0:T(8,128)S(1)} %get-tuple-element.27), kind=kLoop, calls=%fused_computation.13 | loop fusion | flops 6258688 | bytes 4456448 | tf_op jit(solution)/shard_map/rhd,rthd->hrt/dot_general | solution.py:87
  44.2 0.9 fusion.92
  45.2 2.2 fusion.5
  47.5 2.7 fusion.4
  51.1 6.9 %copy.116 = bf16[1,256,64,128]{1,3,2,0:T(8,128)(2,1)} copy(bf16[1,256,64,128]{3,2,1,0:T(8,128)(2,1)} %get-tuple-element.13) | data formatting | bytes 8388608
  58.0 2.0 convolution_convert_fusion.2
  60.0 2.3 copy.115
  62.3 3.2 %multiply_reduce_fusion = f32[256,2,64]{0,2,1:T(8,128)S(1)} fusion(bf16[256,2,64,64]{0,3,1,2:T(8,128)(2,1)} %bitcast.146, f32[256,2,64]{0,1,2:T(2,128)S(1)} %bitcast_convert_fusion), kind=kLoop, calls=%fused_computation.12 | loop fusion | flops 6258688 | bytes 4456448 | tf_op jit(solution)/shard_map/hrt,rthd->rhd/dot_general | solution.py:102
  65.5 5.1 %fusion.19 = bf16[256,2,64]{0,2,1:T(8,128)(2,1)S(1)} fusion(f32[256,2,64]{0,2,1:T(8,128)S(1)} %multiply_reduce_fusion, f32[2,256,8,512]{3,1,2,0:T(8,128)} %copy-done.1, f32[2,256]{1,0:T(2,128)S(1)} %get-tuple-element.11, f32[2,256]{1,0:T(2,128)S(1)} %maximum_maximum_fusion, f32[2,256,512]{2,1,0:T(8,128)S(1)} %copy.78, ...), kind=kOutput, calls=%fused_computation.52 | convolution fusion | flops 281182208 | bytes 11802624 | tf_op jit(solution)/shard_map/hrgj,gjhd->rhd/dot_general | solution.py:101
  71.1 2.6 collective-permute-done
  73.9 0.9 collective-permute-start.1
  74.8 24.4 %collective-permute-done.1 = f32[256,1024]{1,0:T(8,128)S(1)} collective-permute-done((f32[256,1024]{1,0:T(8,128)S(1)}, f32[256,1024]{1,0:T(8,128)S(1)}, u32[]{:S(2)}, u32[]{:S(2)}) %collective-permute-start.1) | collective-permute-done | bytes 1048608 | tf_op jit(solution)/shard_map/ppermute | solution.py:16
  99.4 1.5 collective-permute-start.2
  101.3 1.2 reduce-window.14
  102.9 22.6 %collective-permute-done.2 = f32[256,1024]{1,0:T(8,128)} collective-permute-done((f32[256,1024]{1,0:T(8,128)S(1)}, f32[256,1024]{1,0:T(8,128)}, u32[]{:S(2)}, u32[]{:S(2)}) %collective-permute-start.2) | collective-permute-done | bytes 1048608 | tf_op jit(solution)/shard_map/ppermute | solution.py:16
  125.5 1.5 fusion.24
  127.8 1.2 reshape.353
  129.0 3.2 %convolution_convert_fusion.1 = bf16[640,1024]{1,0:T(8,128)(2,1)} fusion(bf16[512,1024]{1,0:T(8,128)(2,1)} %reshape.353, s32[512]{0:T(512)S(1)} %multiply_add_fusion), kind=kOutput, calls=%fused_computation.28 | convolution fusion | flops 672071680 | bytes 2361344 | tf_op jit(solution)/shard_map/dot_general | solution.py:173
  132.2 8.0 %all-to-all-start = ((bf16[16,40,1024]{2,1,0:T(8,128)(2,1)}), bf16[16,40,1024]{2,1,0:T(8,128)(2,1)S(1)}, u32[]{:S(2)}, u32[]{:S(2)}) async-start(bf16[16,40,1024]{2,1,0:T(8,128)(2,1)} %bitcast.149), calls=%async_computation | async-start | bytes 2621440 | tf_op jit(solution)/shard_map/all_to_all | solution.py:180
  141.6 0.7 convert_reduce_fusion.1
  142.3 1.6 scatter_custom_fusion
  144.6 14.8 %all-to-all-done = bf16[16,40,1024]{2,1,0:T(8,128)(2,1)S(1)} async-done(((bf16[16,40,1024]{2,1,0:T(8,128)(2,1)}), bf16[16,40,1024]{2,1,0:T(8,128)(2,1)S(1)}, u32[]{:S(2)}, u32[]{:S(2)}) %all-to-all-start) | async-done | bytes 1310752 | tf_op jit(solution)/shard_map/all_to_all | solution.py:180
  159.4 2.8 fusion.48
  162.2 4.3 %convolution_convert_fusion = bf16[640,1024]{1,0:T(8,128)(2,1)} fusion(bf16[640,1024]{1,0:T(8,128)(2,1)S(1)} %bitcast.148, f32[640,352]{0,1:T(8,128)} %fusion.48, bf16[1,352,1024]{2,1,0:T(8,128)(2,1)S(1)} %copy-done, bf16[1,1024,352]{1,2,0:T(8,128)(2,1)} %param.37), kind=kOutput, calls=%fused_computation.27 | convolution fusion | flops 925655040 | bytes 4964352 | tf_op jit(solution)/shard_map/dot_general | solution.py:186
  166.5 8.1 %broadcast_select_fusion = bf16[2,256,64,128]{3,2,1,0:T(8,128)(2,1)} fusion(bf16[2,256,64,128]{3,2,1,0:T(8,128)(2,1)} %param.22, pred[256,64]{1,0:T(8,128)(4,1)S(1)} %copy.89, bf16[2,256,128]{2,1,0:T(8,128)(2,1)S(1)} %copy.90), kind=kLoop, calls=%fused_computation.20 | loop fusion | flops 4194304 | bytes 16924672 | tf_op jit(solution)/shard_map/jit(_where)/select_n | solution.py:150
  174.6 4.7 %gather_fusion.3 = bf16[4,2,64,128]{3,2,1,0:T(8,128)(2,1)} fusion(bf16[2,256,64,128]{3,2,1,0:T(8,128)(2,1)} %broadcast_select_fusion, s32[1024]{0:T(1024)S(1)} %pad_clamp_fusion.3), kind=kCustom, calls=%fused_computation.4 | custom fusion | bytes 262160 | tf_op jit(solution)/shard_map/gather | solution.py:216
  179.5 15.5 %scatter_custom_fusion.1 = s32[4096]{0:T(1024)S(1)} fusion(s32[4096]{0:T(1024)S(1)} %add_select_fusion.1, s32[4096]{0:T(1024)S(1)} %iota.80, s32[]{:T(128)} %constant.36.clone.1), kind=kCustom, calls=%fused_computation.136 | custom fusion | bytes 16388 | tf_op jit(solution)/shard_map/scatter | solution.py:206
  195.7 29.4 %all-reduce.2.cloned.1.call-done = bf16[16,40,1024]{2,1,0:T(8,128)(2,1)} async-done(((bf16[16,40,1024]{2,1,0:T(8,128)(2,1)}), bf16[16,40,1024]{2,1,0:T(8,128)(2,1)}) %all-reduce.2.cloned.1.call-update) | async-done | bytes 1310736 | tf_op jit(solution)/shard_map/psum | solution.py:185
  225.1 6.9 %all-to-all-start.1 = ((bf16[16,40,1024]{2,1,0:T(8,128)(2,1)}), bf16[16,40,1024]{2,1,0:T(8,128)(2,1)S(1)}, u32[]{:S(2)}, u32[]{:S(2)}) async-start(bf16[16,40,1024]{2,1,0:T(8,128)(2,1)} %all-reduce.2.cloned.1.call-done), calls=%async_computation.1 | async-start | bytes 2621440 | tf_op jit(solution)/shard_map/all_to_all | solution.py:189
  233.0 2.2 gather_fusion.4
  235.2 2.0 scatter_fusion
  237.2 18.9 %all-to-all-done.1 = bf16[16,40,1024]{2,1,0:T(8,128)(2,1)S(1)} async-done(((bf16[16,40,1024]{2,1,0:T(8,128)(2,1)}), bf16[16,40,1024]{2,1,0:T(8,128)(2,1)S(1)}, u32[]{:S(2)}, u32[]{:S(2)}) %all-to-all-start.1) | async-done | bytes 1310752 | tf_op jit(solution)/shard_map/all_to_all | solution.py:189
  256.1 1.0 fusion.10
  258.0 22.0 %all-gather.1 = bf16[16,4,1024]{2,1,0:T(4,128)(2,1)S(1)} all-gather(bf16[1,4,1024]{2,1,0:T(4,128)(2,1)S(1)} %bitcast.160), channel_id=2, replica_groups=mesh['req'=16,'tp'=8] {'req'}, dimensions={0}, use_global_device_ids=true | all-gather | bytes 139264 | tf_op jit(solution)/shard_map/all_gather | solution.py:218
  280.1 1.0 scatter_custom_fusion.2
  281.1 0.8 copy-done.6
  (111 shorter events, 11.1 us)
Async XLA Ops:
  8.0 154.2 %copy-start = (bf16[1,352,1024]{2,1,0:T(8,128)(2,1)S(1)}, bf16[1,352,1024]{2,1,0:T(8,128)(2,1)}, u32[]{:S(2)}) copy-start(bf16[1,352,1024]{2,1,0:T(8,128)(2,1)} %param.38) | copy-start | bytes 2162692
  14.7 7.1 %copy-start.3 = (bf16[256,1024]{1,0:T(8,128)(2,1)S(1)}, bf16[256,1024]{1,0:T(8,128)(2,1)}, u32[]{:S(2)}) copy-start(bf16[256,1024]{1,0:T(8,128)(2,1)} %param.20) | copy-start | bytes 1572868
  14.8 7.3 %copy-start.2 = (bf16[2,8,512,128]{3,2,1,0:T(8,128)(2,1)S(1)}, bf16[2,8,512,128]{3,2,1,0:T(8,128)(2,1)}, u32[]{:S(2)}) copy-start(bf16[2,8,512,128]{3,2,1,0:T(8,128)(2,1)} %param.21) | copy-start | bytes 6291460
  31.1 7.0 %copy-start.18 = (bf16[1024,128]{1,0:T(8,128)(2,1)S(1)}, bf16[1024,128]{1,0:T(8,128)(2,1)}, u32[]{:S(2)}) copy-start(bf16[1024,128]{1,0:T(8,128)(2,1)} %param.29) | copy-start | bytes 786436
  31.1 7.0 %copy-start.20 = (f32[1024]{0:T(1024)S(1)}, f32[1024]{0:T(1024)}, u32[]{:S(2)}) copy-start(f32[1024]{0:T(1024)} %param.28) | copy-start | bytes 12292
  31.1 7.4 %copy-start.19 = (bf16[1024,128]{1,0:T(8,128)(2,1)S(1)}, bf16[1024,128]{1,0:T(8,128)(2,1)}, u32[]{:S(2)}) copy-start(bf16[1024,128]{1,0:T(8,128)(2,1)} %param.30) | copy-start | bytes 786436
  31.1 8.6 %copy-start.17 = (f32[32,2]{0,1:T(2,128)S(1)}, f32[32,2]{0,1:T(2,128)}, u32[]{:S(2)}) copy-start(f32[32,2]{0,1:T(2,128)} %param.27) | copy-start | bytes 772
  38.1 6.1 %copy-start.10 = (s32[256,64]{0,1:T(8,128)S(1)}, s32[256,64]{0,1:T(8,128)}, u32[]{:S(2)}) copy-start(s32[256,64]{0,1:T(8,128)} %subtract_clamp_fusion.1) | copy-start | bytes 196612
  38.9 6.2 %copy-start.7 = (bf16[256,128]{0,1:T(8,128)(2,1)}, bf16[256,128]{0,1:T(8,128)(2,1)S(1)}, u32[]{:S(2)}) copy-start(bf16[256,128]{0,1:T(8,128)(2,1)S(1)} %convolution_convert_fusion.3) | copy-start | bytes 196612
  39.0 6.2 %copy-start.4 = (bf16[1,8,512,128]{2,3,1,0:T(8,128)(2,1)S(1)}, bf16[1,8,512,128]{2,3,1,0:T(8,128)(2,1)}, u32[]{:S(2)}) copy-start(bf16[1,8,512,128]{2,3,1,0:T(8,128)(2,1)} %copy.113) | copy-start | bytes 3145732
  47.4 3.4 %copy-start.1 = (f32[2,256,8,512]{3,1,2,0:T(8,128)}, f32[2,256,8,512]{3,1,2,0:T(8,128)S(1)}, u32[]{:S(2)}) copy-start(f32[2,256,8,512]{3,1,2,0:T(8,128)S(1)} %get-tuple-element.26) | copy-start | bytes 25165828
  62.3 3.2 %copy-start.5 = (bf16[1,8,512,128]{2,3,1,0:T(8,128)(2,1)S(1)}, bf16[1,8,512,128]{2,3,1,0:T(8,128)(2,1)}, u32[]{:S(2)}) copy-start(bf16[1,8,512,128]{2,3,1,0:T(8,128)(2,1)} %copy.115) | copy-start | bytes 3145732
  62.3 3.2 %copy-start.12 = (bf16[256,128]{0,1:T(8,128)(2,1)S(1)}, bf16[256,128]{0,1:T(8,128)(2,1)}, u32[]{:S(2)}) copy-start(bf16[256,128]{0,1:T(8,128)(2,1)} %convolution_convert_fusion.2) | copy-start | bytes 196612
  65.5 5.2 %copy-start.9 = (bf16[128,1024]{1,0:T(8,128)(2,1)S(1)}, bf16[128,1024]{1,0:T(8,128)(2,1)}, u32[]{:S(2)}) copy-start(bf16[128,1024]{1,0:T(8,128)(2,1)} %param.32) | copy-start | bytes 786436
  70.7 30.2 %copy-start.15 = (s32[256,2]{0,1:T(2,128)S(1)}, s32[256,2]{0,1:T(2,128)}, u32[]{:S(2)}) copy-start(s32[256,2]{0,1:T(2,128)} %param.35) | copy-start | bytes 6148
  71.0 2.7 collective-permute-start
  73.9 53.0 %copy-start.16 = (f32[1024]{0:T(1024)S(1)}, f32[1024]{0:T(1024)}, u32[]{:S(2)}) copy-start(f32[1024]{0:T(1024)} %param.33) | copy-start | bytes 12292
  73.9 25.3 %collective-permute-start.1 = (f32[256,1024]{1,0:T(8,128)S(1)}, f32[256,1024]{1,0:T(8,128)S(1)}, u32[]{:S(2)}, u32[]{:S(2)}) collective-permute-start(f32[256,1024]{1,0:T(8,128)S(1)} %add.188), channel_id=1, source_target_pairs={{0,2},{1,3},{2,0},{3,1},{4,6},{5,7},{6,4},{7,5},{8,10},{9,11},{10,... | collective-permute-start | bytes 3145736 | tf_op jit(solution)/shard_map/ppermute | solution.py:16
  99.4 26.1 %collective-permute-start.2 = (f32[256,1024]{1,0:T(8,128)S(1)}, f32[256,1024]{1,0:T(8,128)}, u32[]{:S(2)}, u32[]{:S(2)}) collective-permute-start(f32[256,1024]{1,0:T(8,128)S(1)} %add.189), channel_id=1, source_target_pairs={{0,4},{1,5},{2,6},{3,7},{4,0},{5,1},{6,2},{7,3},{8,12},{9,13},{10,... | collective-permute-start | bytes 3145736 | tf_op jit(solution)/shard_map/ppermute | solution.py:16
  127.7 12.6 %copy-start.11 = (s32[4096]{0:T(1024)S(1)}, s32[4096]{0:T(1024)}, u32[]{:S(2)}) copy-start(s32[4096]{0:T(1024)} %param.39) | copy-start | bytes 49156
  127.7 13.6 %copy-start.8 = (bf16[256,128]{0,1:T(8,128)(2,1)S(1)}, bf16[256,128]{0,1:T(8,128)(2,1)}, u32[]{:S(2)}) copy-start(bf16[256,128]{0,1:T(8,128)(2,1)} %copy-done.7) | copy-start | bytes 196612
  127.7 13.6 %copy-start.13 = (bf16[256,128]{0,1:T(8,128)(2,1)S(1)}, bf16[256,128]{0,1:T(8,128)(2,1)}, u32[]{:S(2)}) copy-start(bf16[256,128]{0,1:T(8,128)(2,1)} %convolution_convert_fusion.2) | copy-start | bytes 196612
  132.2 27.1 %all-to-all-start = ((bf16[16,40,1024]{2,1,0:T(8,128)(2,1)}), bf16[16,40,1024]{2,1,0:T(8,128)(2,1)S(1)}, u32[]{:S(2)}, u32[]{:S(2)}) async-start(bf16[16,40,1024]{2,1,0:T(8,128)(2,1)} %bitcast.149), calls=%async_computation | async-start | bytes 2621440 | tf_op jit(solution)/shard_map/all_to_all | solution.py:180
  140.3 84.8 %all-reduce.2.cloned.1.call-start = ((), (), s32[]{:S(2)}) async-start(), calls=%async_computation.2 | async-start | bytes 2621440 | tf_op jit(solution)/shard_map/psum | solution.py:185
  166.5 66.6 %all-gather.4.cloned.1.call-start = ((), (), s32[]{:S(2)}) async-start(), calls=%async_computation.3 | async-start | bytes 2228224 | tf_op jit(solution)/shard_map/all_gather | solution.py:219
  174.6 58.1 %copy-start.14 = (bf16[1024,16]{0,1:T(8,128)(2,1)S(1)}, bf16[1024,16]{0,1:T(8,128)(2,1)}, u32[]{:S(2)}) copy-start(bf16[1024,16]{0,1:T(8,128)(2,1)} %param.34) | copy-start | bytes 98308
  225.1 31.0 %all-to-all-start.1 = ((bf16[16,40,1024]{2,1,0:T(8,128)(2,1)}), bf16[16,40,1024]{2,1,0:T(8,128)(2,1)S(1)}, u32[]{:S(2)}, u32[]{:S(2)}) async-start(bf16[16,40,1024]{2,1,0:T(8,128)(2,1)} %all-reduce.2.cloned.1.call-done), calls=%async_computation.1 | async-start | bytes 2621440 | tf_op jit(solution)/shard_map/all_to_all | solution.py:189
  281.1 0.8 copy-start.6
Sparse Core Ops, SparseCore 0:
  166.6 58.4 all-reduce.1
Sparse Core Ops, SparseCore 1:
  179.4 42.3 all-gather.3
